TPU v7x, 32 devices: a whole 2x2x4 slice. The times are simulated.
32 devices in a mesh: snp: 8 (over z, x), trait: 4 (over y, core).
Axes of the slice: x: 2, y: 2, z: 4, core: 2. Of those that a mesh axis runs over, the one named last changes fastest.
Arguments:
- genotype: bfloat16 [32, 8192], P(None, 'snp'), may hold values from -0.0625 to 0.0625
- targets: bfloat16 [32, 16384], P('snp', 'trait'), may hold values from -6 to 6
- effect_sizes: float32 [8192, 16384], P('snp', 'trait'), may hold values from -6 to 6
- membership: int32 [4, 128, 128], replicated, may hold values from 0 to 1, as said below
- node_weight: float32 [4, 128], replicated, may hold values from 0.03 to 1
Outputs:
- updated: float32 [8192, 16384], P('snp', 'trait')
Inputs may be any that keep to these rules, and one draw needn't show every extreme that they name: `membership`: at each level the node slots 0 .. c - 1 partition all 128 trait blocks, the remaining slots cover none; every node of a level lies inside one node of the next level; at level 0 each block is its own node.
All inputs are finite; a program needn't handle non-finite values.
Results may differ from a plain program's by a relative error of at most 0.00042.
Values may be sent and summed in bfloat16 or wider, within the bound.
A program may use at most 128 MiB of HBM per device.

v0:
```python
import jax
import jax.numpy as jnp
from jax import lax
from jax.sharding import PartitionSpec as P

TB = 128
LEVELS = 4
step_size = 0.5


def factor_of(node_sq, threshold):
    norm = jnp.sqrt(node_sq)
    return jnp.maximum(norm - threshold, 0.0) / jnp.maximum(norm, threshold)


def shrink_local(value, membership, node_weight):
    local_blocks = value.shape[1] // TB
    first_block = lax.axis_index("trait") * local_blocks
    for level in range(LEVELS):
        member_all = membership[level].astype(jnp.float32)
        count = jnp.sum(member_all, axis=1)
        threshold = step_size * node_weight[level] * jnp.sqrt(TB * jnp.maximum(count, 1.0))
        member = lax.dynamic_slice_in_dim(member_all, first_block, local_blocks, 1)
        blocks = value.reshape(value.shape[0], local_blocks, TB)
        block_sq = jnp.sum(blocks * blocks, axis=2)
        partial_sq = jnp.dot(block_sq, member.T, precision=lax.Precision.HIGHEST)
        node_sq = lax.psum(partial_sq, "trait")
        factor = factor_of(node_sq, threshold)
        block_factor = jnp.dot(factor, member, precision=lax.Precision.HIGHEST)
        value = (blocks * block_factor[:, :, None]).reshape(value.shape)
    return value


def body(genotype, targets, effect_sizes, membership, node_weight):
    current = effect_sizes
    targets_full = lax.all_gather(targets, "snp", axis=0, tiled=True)
    current_bf = current.astype(jnp.bfloat16)
    fitted = lax.psum(jnp.dot(genotype, current_bf, preferred_element_type=jnp.float32), "snp")
    residual = (targets_full.astype(jnp.float32) - fitted).astype(jnp.bfloat16)
    gradient = lax.dot_general(
        genotype, residual, (((0,), (0,)), ((), ())), preferred_element_type=jnp.float32
    )
    current = shrink_local(current + step_size * gradient, membership, node_weight)
    return current


def solution(mesh):
    return jax.shard_map(
        body,
        mesh=mesh,
        in_specs=(P(None, "snp"), P("snp", "trait"), P("snp", "trait"), P(), P()),
        out_specs=P("snp", "trait"),
        check_vma=False,
    )
```

profile of v0, /device:TPU:0, one launch (start us, length us, event | category | flops | bytes accessed | tf_op | source)
XLA Modules:
  0.0 313.8 jit_solution(9431012328404320103)
XLA Ops:
  6.5 0.8 copy-done
  7.4 8.1 %fusion = f32[32,4096]{1,0:T(8,128)} fusion(bf16[32,1024]{1,0:T(8,128)(2,1)S(1)} %copy-done, f32[1024,4096]{1,0:T(8,128)} %param.7), kind=kOutput, calls=%fused_computation.9 | convolution fusion | flops 272629760 | bytes 17367040 | tf_op jit(solution)/shard_map/dot_general | solution.py:38
  15.5 0.0 all-reduce.6.cloned.1.call-update
  15.5 0.0 all-reduce.8.cloned.1.call-start
  15.6 17.5 %copy.8 = f32[1024,4096]{0,1:T(8,128)} copy(f32[1024,4096]{1,0:T(8,128)} %param.7) | data formatting | bytes 33554432 | tf_op args[2]
  33.1 32.6 %all-gather = bf16[8,4,4096]{2,1,0:T(4,128)(2,1)S(1)} all-gather(bf16[1,4,4096]{2,1,0:T(4,128)(2,1)S(1)} %bitcast.72), channel_id=1, replica_groups=mesh['snp'=8,'trait'=4] {'snp'}, dimensions={0}, use_global_device_ids=true | all-gather | bytes 294912 | tf_op jit(solution)/shard_map/all_gather | solution.py:36
  65.8 25.0 %all-reduce.6.cloned.1.call-done = f32[32,4096]{1,0:T(8,128)} async-done(((f32[32,4096]{1,0:T(8,128)}), f32[32,4096]{1,0:T(8,128)}) %all-reduce.6.cloned.1.call-update) | async-done | bytes 524304 | tf_op jit(solution)/shard_map/psum | solution.py:38
  90.8 11.0 %multiply_reduce_fusion.3 = (f32[1024,32]{0,1:T(8,128)S(1)}, f32[1024,4096]{0,1:T(8,128)}) fusion(f32[1024,4096]{0,1:T(8,128)} %copy.8, bf16[32,1024]{1,0:T(8,128)(2,1)S(1)} %copy-done, f32[32,4096]{1,0:T(8,128)S(1)} %reshape.95, f32[32,4096]{1,0:T(8,128)} %all-reduce.6.cloned.1.call-done), kind=kOutput, calls=%fused_computation.8 | convolution fusion | flops 285442048 | bytes 34799616 | tf_op jit(solution)/shard_map/dot_general | solution.py:40
  101.8 1.8 fusion.24
  103.7 0.0 all-reduce.8.cloned.1.call-update
  103.7 0.0 all-reduce.10.cloned.1.call-start
  103.8 0.1 fusion.53
  103.9 32.4 %all-reduce.8.cloned.1.call-done = f32[1024,128]{1,0:T(8,128)} async-done(((f32[1024,128]{1,0:T(8,128)}), f32[1024,128]{1,0:T(8,128)}) %all-reduce.8.cloned.1.call-update) | async-done | bytes 524304 | tf_op jit(solution)/shard_map/psum | solution.py:27
  136.3 1.8 fusion.2
  138.2 8.5 %multiply_reduce_fusion.2 = f32[1024,32]{0,1:T(8,128)S(1)} fusion(f32[1024,4096]{0,1:T(8,128)} %get-tuple-element.18, f32[1024,32]{0,1:T(8,128)S(1)} %fusion.2), kind=kLoop, calls=%fused_computation.7 | loop fusion | flops 12550144 | bytes 17039360 | tf_op jit(solution)/shard_map/reduce_sum | solution.py:25
  146.7 1.9 fusion.21
  148.6 0.2 all-reduce.12.cloned.1.call-start
  148.8 33.1 %all-reduce.10.cloned.1.call-done = f32[1024,128]{1,0:T(8,128)} async-done(((f32[1024,128]{1,0:T(8,128)}), f32[1024,128]{1,0:T(8,128)}) %all-reduce.10.cloned.1.call-update) | async-done | bytes 524304 | tf_op jit(solution)/shard_map/psum | solution.py:27
  181.9 1.8 fusion.3
  183.7 9.5 %multiply_reduce_fusion.1 = f32[1024,32]{0,1:T(8,128)S(1)} fusion(f32[1024,4096]{0,1:T(8,128)} %get-tuple-element.18, f32[1024,32]{0,1:T(8,128)S(1)} %fusion.3, f32[1024,32]{0,1:T(8,128)S(1)} %fusion.2), kind=kLoop, calls=%fused_computation.6 | loop fusion | flops 16744448 | bytes 17170432 | tf_op jit(solution)/shard_map/reduce_sum | solution.py:25
  193.2 1.9 fusion.18
  195.1 0.0 all-reduce.12.cloned.1.call-update
  195.1 0.3 all-reduce.14.cloned.1.call-start
  195.4 33.1 %all-reduce.12.cloned.1.call-done = f32[1024,128]{1,0:T(8,128)} async-done(((f32[1024,128]{1,0:T(8,128)}), f32[1024,128]{1,0:T(8,128)}) %all-reduce.12.cloned.1.call-update) | async-done | bytes 524304 | tf_op jit(solution)/shard_map/psum | solution.py:27
  228.4 1.8 fusion.4
  230.2 10.6 %multiply_reduce_fusion = f32[1024,32]{0,1:T(8,128)S(1)} fusion(f32[1024,4096]{0,1:T(8,128)} %get-tuple-element.18, f32[1024,32]{0,1:T(8,128)S(1)} %fusion.4, f32[1024,32]{0,1:T(8,128)S(1)} %fusion.3, f32[1024,32]{0,1:T(8,128)S(1)} %fusion.2), kind=kLoop, calls=%fused_computation.5 | loop fusion | flops 20938752 | bytes 17301504 | tf_op jit(solution)/shard_map/reduce_sum | solution.py:25
  240.8 1.9 fusion.15
  242.7 0.0 all-reduce.14.cloned.1.call-update
  242.7 33.3 %all-reduce.14.cloned.1.call-done = f32[1024,128]{1,0:T(8,128)} async-done(((f32[1024,128]{1,0:T(8,128)}), f32[1024,128]{1,0:T(8,128)}) %all-reduce.14.cloned.1.call-update) | async-done | bytes 524304 | tf_op jit(solution)/shard_map/psum | solution.py:27
  276.0 1.8 fusion.5
  277.9 12.0 %bitcast_multiply_fusion = f32[1024,4096]{0,1:T(8,128)} fusion(f32[1024,4096]{0,1:T(8,128)} %get-tuple-element.18, f32[1024,32]{0,1:T(8,128)S(1)} %fusion.5, f32[1024,32]{0,1:T(8,128)S(1)} %fusion.4, f32[1024,32]{0,1:T(8,128)S(1)} %fusion.3, f32[1024,32]{0,1:T(8,128)S(1)} %fusion.2), kind=kLoop, calls=%fused_computation | loop fusion | flops 16777216 | bytes 34078720 | tf_op jit(solution)/shard_map/mul | solution.py:30
  289.9 17.4 %copy.9 = f32[1024,4096]{1,0:T(8,128)} copy(f32[1024,4096]{0,1:T(8,128)} %bitcast_multiply_fusion) | data formatting | bytes 33554432 | tf_op jit(solution)/shard_map/mul | solution.py:30
  (14 shorter events, 0.1 us)
Async XLA Ops:
  6.5 0.8 copy-start
  6.5 84.3 %all-reduce.6.cloned.1.call-start = ((), (), s32[]{:S(2)}) async-start(), calls=%async_computation | async-start | bytes 1048576 | tf_op jit(solution)/shard_map/psum | solution.py:38
  15.5 120.8 %all-reduce.8.cloned.1.call-start = ((), (), s32[]{:S(2)}) async-start(), calls=%async_computation.1 | async-start | bytes 1048576 | tf_op jit(solution)/shard_map/psum | solution.py:27
  15.6 17.5 %copy-start.3 = (bf16[4,4096]{1,0:T(4,128)(2,1)S(1)}, bf16[4,4096]{1,0:T(4,128)(2,1)}, u32[]{:S(2)}) copy-start(bf16[4,4096]{1,0:T(4,128)(2,1)} %param.6) | copy-start | bytes 98308
  15.6 50.2 %copy-start.2 = (s32[4,128,128]{2,1,0:T(8,128)S(1)}, s32[4,128,128]{2,1,0:T(8,128)}, u32[]{:S(2)}) copy-start(s32[4,128,128]{2,1,0:T(8,128)} %param.8) | copy-start | bytes 786436
  65.8 38.1 %copy-start.4 = (f32[4,128]{1,0:T(4,128)S(1)}, f32[4,128]{1,0:T(4,128)}, u32[]{:S(2)}) copy-start(f32[4,128]{1,0:T(4,128)} %param.9) | copy-start | bytes 6148
  103.7 78.2 %all-reduce.10.cloned.1.call-start = ((), (), s32[]{:S(2)}) async-start(), calls=%async_computation.2 | async-start | bytes 1048576 | tf_op jit(solution)/shard_map/psum | solution.py:27
  148.6 79.8 %all-reduce.12.cloned.1.call-start = ((), (), s32[]{:S(2)}) async-start(), calls=%async_computation.3 | async-start | bytes 1048576 | tf_op jit(solution)/shard_map/psum | solution.py:27
  195.1 80.9 %all-reduce.14.cloned.1.call-start = ((), (), s32[]{:S(2)}) async-start(), calls=%async_computation.4 | async-start | bytes 1048576 | tf_op jit(solution)/shard_map/psum | solution.py:27
  277.9 29.4 %copy-start.1 = (bf16[32,1024]{1,0:T(8,128)(2,1)S(1)}, bf16[32,1024]{1,0:T(8,128)(2,1)}, u32[]{:S(2)}) copy-start(bf16[32,1024]{1,0:T(8,128)(2,1)} %param.5) | copy-start | bytes 196612
Sparse Core Ops, SparseCore 0:
  15.6 75.1 all-reduce.5
  103.8 32.4 all-reduce.7
  148.7 33.1 all-reduce.9
  195.2 33.1 all-reduce.11
  242.8 33.1 all-reduce.13
where the time goes:
time: 315 us; the launch traced here: 314 us
  waiting for transfers between devices  157 us (50%)
  other arithmetic  40.7 us (13%)
  local copies, waits for them, and re-layouts  35.8 us (11%)
  matrix products  33.9 us (11%)
  blocking collectives  32.6 us (10%)
  between operations  13.3 us (4%)
    psum x4, waiting for transfers between devices, shrink_local(): node_sq = lax.psum(partial_sq, 'trait')  132 us
    all_gather x1, blocking collectives, body(): targets_full = lax.all_gather(targets, 'snp', axis=0, tiled=True)  32.6 us
    reduce_sum x3, other arithmetic, shrink_local(): block_sq = jnp.sum(blocks * blocks, axis=2)  28.6 us
    psum x1, waiting for transfers between devices, body(): lax.psum(jnp.dot(genotype, current_bf, preferred_element_type=jnp.float32...  25 us
    unnamed x11, local copies, waits for them, and re-layouts  18.4 us
    mul x1, local copies, waits for them, and re-layouts, shrink_local(): value = (blocks * block_factor[:, :, None]).reshape(value.shape)  17.4 us
    mul x1, other arithmetic, shrink_local(): value = (blocks * block_factor[:, :, None]).reshape(value.shape)  12 us
    dot_general x1, matrix products, body(): lax.dot_general(genotype, residual, (((0,), (0,)), ((), ())), preferred_e...  11 us
  transfers between devices with their start and end apart: 5, of which 5 were waited for; matrix products, arithmetic and copies ran while one was open for 6% of the time, Pallas kernels for 0%

commit v1 on v0

--- a/solution.py
+++ b/solution.py
@@ -24,7 +24,11 @@
         blocks = value.reshape(value.shape[0], local_blocks, TB)
         block_sq = jnp.sum(blocks * blocks, axis=2)
         partial_sq = jnp.dot(block_sq, member.T, precision=lax.Precision.HIGHEST)
-        node_sq = lax.psum(partial_sq, "trait")
+        node_sq = partial_sq
+        for hop in (1, 2):
+            node_sq = node_sq + lax.ppermute(
+                node_sq, "trait", [(dev, dev ^ hop) for dev in range(4)]
+            )
         factor = factor_of(node_sq, threshold)
         block_factor = jnp.dot(factor, member, precision=lax.Precision.HIGHEST)
         value = (blocks * block_factor[:, :, None]).reshape(value.shape)

time: 315 us -> 239 us (0.76)
  waiting for transfers between devices: 157 us -> 82.4 us
  matrix products: 33.9 us -> 26.9 us
  starting transfers between devices: 0.57 us -> 6.44 us
    psum x4 -> x0, waiting for transfers between devices: 132 us -> none  [shrink_local(): node_sq = lax.psum(partial_sq, 'trait')]
    ppermute x0 -> x8, waiting for transfers between devices: none -> 57.4 us  [shrink_local(): lax.ppermute(node_sq, 'trait', [(dev, dev ^ hop) for dev in range(4)])]
    ppermute x0 -> x8, starting transfers between devices: none -> 6.44 us  [shrink_local(): lax.ppermute(node_sq, 'trait', [(dev, dev ^ hop) for dev in range(4)])]
    dot_general x4, matrix products: 7.32 us -> 3.57 us  [shrink_local(): block_factor = jnp.dot(factor, member, precision=lax.Precision.HIGHEST)]
    dot_general x4, matrix products: 7.41 us -> 4.15 us  [shrink_local(): partial_sq = jnp.dot(block_sq, member.T, precision=lax.Precision.HIGHEST)]
  transfers between devices with their start and end apart: 5 -> 9, of which waited for: 5 -> 9; matrix products, arithmetic and copies ran while one was open for 6% -> 7% of each run, Pallas kernels for 0% -> 0%
where the time goes in v1:
time: 239 us
  waiting for transfers between devices  82.4 us (34%)
  other arithmetic  41 us (17%)
  local copies, waits for them, and re-layouts  35.9 us (15%)
  blocking collectives  32.6 us (14%)
  matrix products  26.9 us (11%)
  between operations  13.6 us (6%)
  starting transfers between devices  6.44 us (3%)
    ppermute x8, waiting for transfers between devices, shrink_local(): lax.ppermute(node_sq, 'trait', [(dev, dev ^ hop) for dev in range(4)])  57.4 us
    all_gather x1, blocking collectives, body(): targets_full = lax.all_gather(targets, 'snp', axis=0, tiled=True)  32.6 us
    reduce_sum x3, other arithmetic, shrink_local(): block_sq = jnp.sum(blocks * blocks, axis=2)  28.6 us
    psum x1, waiting for transfers between devices, body(): lax.psum(jnp.dot(genotype, current_bf, preferred_element_type=jnp.float32...  25 us
    unnamed x11, local copies, waits for them, and re-layouts  18.4 us
    mul x1, local copies, waits for them, and re-layouts, shrink_local(): value = (blocks * block_factor[:, :, None]).reshape(value.shape)  17.4 us
    mul x1, other arithmetic, shrink_local(): value = (blocks * block_factor[:, :, None]).reshape(value.shape)  12 us
    dot_general x1, matrix products, body(): lax.dot_general(genotype, residual, (((0,), (0,)), ((), ())), preferred_e...  11 us
  transfers between devices with their start and end apart: 9, of which 9 were waited for; matrix products, arithmetic and copies ran while one was open for 7% of the time, Pallas kernels for 0%

profile of v1, /device:TPU:0, one launch (start us, length us, event | category | flops | bytes accessed | tf_op | source)
XLA Modules:
  0.0 238.7 jit_solution(5376613076420785456)
XLA Ops:
  6.5 0.8 copy-done
  7.4 8.1 %fusion = f32[32,4096]{1,0:T(8,128)} fusion(bf16[32,1024]{1,0:T(8,128)(2,1)S(1)} %copy-done, f32[1024,4096]{1,0:T(8,128)} %param.7), kind=kOutput, calls=%fused_computation.9 | convolution fusion | flops 272629760 | bytes 17367040 | tf_op jit(solution)/shard_map/dot_general | solution.py:42
  15.6 17.5 %copy.8 = f32[1024,4096]{0,1:T(8,128)} copy(f32[1024,4096]{1,0:T(8,128)} %param.7) | data formatting | bytes 33554432 | tf_op args[2]
  33.1 32.6 %all-gather = bf16[8,4,4096]{2,1,0:T(4,128)(2,1)S(1)} all-gather(bf16[1,4,4096]{2,1,0:T(4,128)(2,1)S(1)} %bitcast.72), channel_id=1, replica_groups=mesh['snp'=8,'trait'=4] {'snp'}, dimensions={0}, use_global_device_ids=true | all-gather | bytes 294912 | tf_op jit(solution)/shard_map/all_gather | solution.py:40
  65.8 25.0 %all-reduce.2.cloned.1.call-done = f32[32,4096]{1,0:T(8,128)} async-done(((f32[32,4096]{1,0:T(8,128)}), f32[32,4096]{1,0:T(8,128)}) %all-reduce.2.cloned.1.call-update) | async-done | bytes 524304 | tf_op jit(solution)/shard_map/psum | solution.py:42
  90.8 11.0 %multiply_reduce_fusion.3 = (f32[1024,32]{0,1:T(8,128)S(1)}, f32[1024,4096]{0,1:T(8,128)}) fusion(f32[1024,4096]{0,1:T(8,128)} %copy.8, bf16[32,1024]{1,0:T(8,128)(2,1)S(1)} %copy-done, f32[32,4096]{1,0:T(8,128)S(1)} %reshape.95, f32[32,4096]{1,0:T(8,128)} %all-reduce.2.cloned.1.call-done), kind=kOutput, calls=%fused_computation.8 | convolution fusion | flops 285442048 | bytes 34799616 | tf_op jit(solution)/shard_map/dot_general | solution.py:44
  101.8 1.0 fusion.24
  102.9 1.9 collective-permute-done
  104.9 1.5 collective-permute-start.1
  106.4 0.1 fusion.53
  106.6 12.3 %collective-permute-done.1 = f32[1024,128]{1,0:T(8,128)S(1)} collective-permute-done((f32[1024,128]{1,0:T(8,128)S(1)}, f32[1024,128]{1,0:T(8,128)S(1)}, u32[]{:S(2)}, u32[]{:S(2)}) %collective-permute-start.1) | collective-permute-done | bytes 524320 | tf_op jit(solution)/shard_map/ppermute | solution.py:29
  118.9 0.8 fusion.2
  119.8 8.5 %multiply_reduce_fusion.2 = f32[1024,32]{0,1:T(8,128)S(1)} fusion(f32[1024,4096]{0,1:T(8,128)} %get-tuple-element.18, f32[1024,32]{0,1:T(8,128)S(1)} %fusion.2), kind=kLoop, calls=%fused_computation.7 | loop fusion | flops 12550144 | bytes 17039360 | tf_op jit(solution)/shard_map/reduce_sum | solution.py:25
  128.3 1.0 fusion.21
  129.4 1.9 collective-permute-done.2
  131.4 1.5 collective-permute-start.3
  132.9 12.5 %collective-permute-done.3 = f32[1024,128]{1,0:T(8,128)S(1)} collective-permute-done((f32[1024,128]{1,0:T(8,128)S(1)}, f32[1024,128]{1,0:T(8,128)S(1)}, u32[]{:S(2)}, u32[]{:S(2)}) %collective-permute-start.3) | collective-permute-done | bytes 524320 | tf_op jit(solution)/shard_map/ppermute | solution.py:29
  145.4 0.8 fusion.3
  146.2 9.5 %multiply_reduce_fusion.1 = f32[1024,32]{0,1:T(8,128)S(1)} fusion(f32[1024,4096]{0,1:T(8,128)} %get-tuple-element.18, f32[1024,32]{0,1:T(8,128)S(1)} %fusion.3, f32[1024,32]{0,1:T(8,128)S(1)} %fusion.2), kind=kLoop, calls=%fused_computation.6 | loop fusion | flops 16744448 | bytes 17170432 | tf_op jit(solution)/shard_map/reduce_sum | solution.py:25
  155.7 1.0 fusion.18
  156.8 1.9 collective-permute-done.4
  158.8 1.5 collective-permute-start.5
  160.3 12.5 %collective-permute-done.5 = f32[1024,128]{1,0:T(8,128)S(1)} collective-permute-done((f32[1024,128]{1,0:T(8,128)S(1)}, f32[1024,128]{1,0:T(8,128)S(1)}, u32[]{:S(2)}, u32[]{:S(2)}) %collective-permute-start.5) | collective-permute-done | bytes 524320 | tf_op jit(solution)/shard_map/ppermute | solution.py:29
  172.8 1.1 fusion.4
  173.9 10.6 %multiply_reduce_fusion = f32[1024,32]{0,1:T(8,128)S(1)} fusion(f32[1024,4096]{0,1:T(8,128)} %get-tuple-element.18, f32[1024,32]{0,1:T(8,128)S(1)} %fusion.4, f32[1024,32]{0,1:T(8,128)S(1)} %fusion.3, f32[1024,32]{0,1:T(8,128)S(1)} %fusion.2), kind=kLoop, calls=%fused_computation.5 | loop fusion | flops 20938752 | bytes 17301504 | tf_op jit(solution)/shard_map/reduce_sum | solution.py:25
  184.5 1.0 fusion.15
  185.6 1.9 collective-permute-done.6
  187.6 1.5 collective-permute-start.7
  189.1 12.5 %collective-permute-done.7 = f32[1024,128]{1,0:T(8,128)S(1)} collective-permute-done((f32[1024,128]{1,0:T(8,128)S(1)}, f32[1024,128]{1,0:T(8,128)S(1)}, u32[]{:S(2)}, u32[]{:S(2)}) %collective-permute-start.7) | collective-permute-done | bytes 524320 | tf_op jit(solution)/shard_map/ppermute | solution.py:29
  201.6 0.8 fusion.5
  202.4 12.0 %bitcast_multiply_fusion = f32[1024,4096]{0,1:T(8,128)} fusion(f32[1024,4096]{0,1:T(8,128)} %get-tuple-element.18, f32[1024,32]{0,1:T(8,128)S(1)} %fusion.5, f32[1024,32]{0,1:T(8,128)S(1)} %fusion.4, f32[1024,32]{0,1:T(8,128)S(1)} %fusion.3, f32[1024,32]{0,1:T(8,128)S(1)} %fusion.2), kind=kLoop, calls=%fused_computation | loop fusion | flops 16777216 | bytes 34078720 | tf_op jit(solution)/shard_map/mul | solution.py:34
  214.4 17.4 %copy.9 = f32[1024,4096]{1,0:T(8,128)} copy(f32[1024,4096]{0,1:T(8,128)} %bitcast_multiply_fusion) | data formatting | bytes 33554432 | tf_op jit(solution)/shard_map/mul | solution.py:34
  (22 shorter events, 0.6 us)
Async XLA Ops:
  6.5 0.8 copy-start
  6.5 84.2 %all-reduce.2.cloned.1.call-start = ((), (), s32[]{:S(2)}) async-start(), calls=%async_computation | async-start | bytes 1048576 | tf_op jit(solution)/shard_map/psum | solution.py:42
  15.5 17.6 %copy-start.3 = (bf16[4,4096]{1,0:T(4,128)(2,1)S(1)}, bf16[4,4096]{1,0:T(4,128)(2,1)}, u32[]{:S(2)}) copy-start(bf16[4,4096]{1,0:T(4,128)(2,1)} %param.6) | copy-start | bytes 98308
  15.5 50.2 %copy-start.2 = (s32[4,128,128]{2,1,0:T(8,128)S(1)}, s32[4,128,128]{2,1,0:T(8,128)}, u32[]{:S(2)}) copy-start(s32[4,128,128]{2,1,0:T(8,128)} %param.8) | copy-start | bytes 786436
  65.8 40.8 %copy-start.4 = (f32[4,128]{1,0:T(4,128)S(1)}, f32[4,128]{1,0:T(4,128)}, u32[]{:S(2)}) copy-start(f32[4,128]{1,0:T(4,128)} %param.9) | copy-start | bytes 6148
  102.8 2.0 collective-permute-start
  104.9 14.0 %collective-permute-start.1 = (f32[1024,128]{1,0:T(8,128)S(1)}, f32[1024,128]{1,0:T(8,128)S(1)}, u32[]{:S(2)}, u32[]{:S(2)}) collective-permute-start(f32[1024,128]{1,0:T(8,128)S(1)} %add.37), channel_id=1, source_target_pairs={{0,2},{1,3},{2,0},{3,1},{4,6},{5,7},{6,4},{7,5},{8,10},{9,11},{10,... | collective-permute-start | bytes 1572872 | tf_op jit(solution)/shard_map/ppermute | solution.py:29
  129.3 2.0 collective-permute-start.2
  131.4 14.0 %collective-permute-start.3 = (f32[1024,128]{1,0:T(8,128)S(1)}, f32[1024,128]{1,0:T(8,128)S(1)}, u32[]{:S(2)}, u32[]{:S(2)}) collective-permute-start(f32[1024,128]{1,0:T(8,128)S(1)} %add.39), channel_id=1, source_target_pairs={{0,2},{1,3},{2,0},{3,1},{4,6},{5,7},{6,4},{7,5},{8,10},{9,11},{10,... | collective-permute-start | bytes 1572872 | tf_op jit(solution)/shard_map/ppermute | solution.py:29
  156.8 2.0 collective-permute-start.4
  158.8 14.0 %collective-permute-start.5 = (f32[1024,128]{1,0:T(8,128)S(1)}, f32[1024,128]{1,0:T(8,128)S(1)}, u32[]{:S(2)}, u32[]{:S(2)}) collective-permute-start(f32[1024,128]{1,0:T(8,128)S(1)} %add.41), channel_id=1, source_target_pairs={{0,2},{1,3},{2,0},{3,1},{4,6},{5,7},{6,4},{7,5},{8,10},{9,11},{10,... | collective-permute-start | bytes 1572872 | tf_op jit(solution)/shard_map/ppermute | solution.py:29
  185.5 2.0 collective-permute-start.6
  187.6 14.0 %collective-permute-start.7 = (f32[1024,128]{1,0:T(8,128)S(1)}, f32[1024,128]{1,0:T(8,128)S(1)}, u32[]{:S(2)}, u32[]{:S(2)}) collective-permute-start(f32[1024,128]{1,0:T(8,128)S(1)} %add.43), channel_id=1, source_target_pairs={{0,2},{1,3},{2,0},{3,1},{4,6},{5,7},{6,4},{7,5},{8,10},{9,11},{10,... | collective-permute-start | bytes 1572872 | tf_op jit(solution)/shard_map/ppermute | solution.py:29
  202.4 29.4 %copy-start.1 = (bf16[32,1024]{1,0:T(8,128)(2,1)S(1)}, bf16[32,1024]{1,0:T(8,128)(2,1)}, u32[]{:S(2)}) copy-start(bf16[32,1024]{1,0:T(8,128)(2,1)} %param.5) | copy-start | bytes 196612
Sparse Core Ops, SparseCore 0:
  15.6 75.0 all-reduce.1
